TPU v7x, 128 devices: a whole 4x4x4 slice. The times are simulated.
128 devices in a mesh: tm: 16 (over z, y_hi, core), space: 8 (over x, y_lo).
Axes of the slice: x: 4, y: 4 (y_hi: 2, y_lo: 2; y = y_hi * 2 + y_lo), z: 4, core: 2. Of those that a mesh axis runs over, the one named last changes fastest.
Arguments:
- tokens: bfloat16 [1, 32, 1024, 1536], P(None, 'tm', 'space'), may hold values from -6 to 6
- grad_out: bfloat16 [1, 32, 1024, 1536], P(None, 'tm', 'space'), may hold values from -6 to 6
- temporal_query: bfloat16 [1536, 768], replicated
- temporal_key: bfloat16 [1536, 768], replicated
- temporal_value: bfloat16 [1536, 768], replicated, may hold values from -0.15625 to 0.15625
- temporal_out: bfloat16 [768, 1536], replicated, may hold values from -0.21875 to 0.21875
- spatial_query: bfloat16 [1536, 768], replicated
- spatial_key: bfloat16 [1536, 768], replicated
- spatial_value: bfloat16 [1536, 768], replicated, may hold values from -0.15625 to 0.15625
- spatial_out: bfloat16 [768, 1536], replicated, may hold values from -0.21875 to 0.21875
Outputs:
- grad_in: bfloat16 [1, 32, 1024, 1536], P(None, 'tm', 'space')
All inputs are finite; a program needn't handle non-finite values.
Results may differ from a plain program's by a relative error of at most 0.025.
Values may be sent and summed in bfloat16 or wider, within the bound.
A program may use at most 192 MiB of HBM per device.

v0:
```python
import jax
import jax.numpy as jnp
from jax import lax
from jax.sharding import PartitionSpec as P

HEADS = 6
HD = 128


EPSILON = 1e-05
TEMPORAL = ("blghe", "bmghe")
SPATIAL = ("bglhe", "bgmhe")


def layer_stats(values):
    centre = jnp.mean(values, axis=-1, keepdims=True)
    spread = jnp.mean(jnp.square(values - centre), axis=-1, keepdims=True)
    inverse = lax.rsqrt(spread + EPSILON)
    return ((values - centre) * inverse, inverse)


def norm_grad(normed, inverse, upstream):
    first_mean = jnp.mean(upstream, axis=-1, keepdims=True)
    cross_mean = jnp.mean(upstream * normed, axis=-1, keepdims=True)
    return inverse * (upstream - first_mean - normed * cross_mean)


def project(inputs, weight):
    joined = inputs.reshape(-1, inputs.shape[-1])
    result = jnp.dot(joined, weight, preferred_element_type=jnp.float32).astype(jnp.bfloat16)
    return result.reshape(inputs.shape[:-1] + (weight.shape[1],))


def back_project(members, weights):
    summed = None
    for member, weight in zip(members, weights):
        joined = member.reshape(-1, HEADS * HD)
        term = jnp.dot(joined, weight.T, preferred_element_type=jnp.float32)
        summed = term if summed is None else summed + term
    return summed.astype(jnp.bfloat16).reshape(members[0].shape[:-2] + (weights[0].shape[0],))


def split_heads(values):
    return values.reshape(values.shape[:-1] + (HEADS, HD))


def merge_heads(values):
    return values.reshape(values.shape[:-2] + (HEADS * HD,))


def product(einsum_form, left, right):
    return jnp.einsum(einsum_form, left, right, preferred_element_type=jnp.float32)


def score_table(queries, key_rows, pattern):
    return product(pattern[0] + "," + pattern[1] + "->bghlm", queries, key_rows) * HD ** (-0.5)


def attend(queries, key_rows, value_rows, pattern):
    scores = score_table(queries, key_rows, pattern)
    row_top = jnp.max(scores, axis=-1, keepdims=True)
    logsum = row_top[..., 0] + jnp.log(jnp.sum(jnp.exp(scores - row_top), axis=-1))
    shares = jnp.exp(scores - logsum[..., None]).astype(jnp.bfloat16)
    blended = product("bghlm," + pattern[1] + "->" + pattern[0], shares, value_rows).astype(
        jnp.bfloat16
    )
    return (blended, logsum)


def offsets(grad_mix, blended, pattern):
    return product(pattern[0] + "," + pattern[0] + "->bghl", grad_mix, blended)


def score_grads(queries, key_rows, value_rows, grad_mix, logsum, offset, pattern):
    scores = score_table(queries, key_rows, pattern)
    shares = jnp.exp(scores - logsum[..., None])
    grad_shares = product(pattern[0] + "," + pattern[1] + "->bghlm", grad_mix, value_rows)
    grad_scores = (shares * (grad_shares - offset[..., None]) * HD ** (-0.5)).astype(jnp.bfloat16)
    return (shares.astype(jnp.bfloat16), grad_scores)


def query_grad(grad_scores, key_rows, pattern):
    return product("bghlm," + pattern[1] + "->" + pattern[0], grad_scores, key_rows).astype(
        jnp.bfloat16
    )


def key_grads(shares, grad_scores, queries, grad_mix, pattern):
    key_form = "bghlm," + pattern[0] + "->" + pattern[1]
    grad_key = product(key_form, grad_scores, queries).astype(jnp.bfloat16)
    grad_value = product(key_form, shares, grad_mix).astype(jnp.bfloat16)
    return (grad_key, grad_value)


def on_device(
    tokens,
    grad_out,
    temporal_query,
    temporal_key,
    temporal_value,
    temporal_out,
    spatial_query,
    spatial_key,
    spatial_value,
    spatial_out,
):
    source = tokens.astype(jnp.float32)
    normed_in, inverse_in = layer_stats(source)
    first_rows = normed_in.astype(jnp.bfloat16)
    time_query = split_heads(project(first_rows, temporal_query))
    time_key = split_heads(project(first_rows, temporal_key))
    time_value = split_heads(project(first_rows, temporal_value))
    time_keys, time_values = (
        lax.all_gather(time_key, "tm", axis=1, tiled=True),
        lax.all_gather(time_value, "tm", axis=1, tiled=True),
    )
    time_blend, time_logsum = attend(time_query, time_keys, time_values, TEMPORAL)
    time_branch = project(merge_heads(time_blend), temporal_out)
    middle = source + time_branch.astype(jnp.float32)
    normed_mid, inverse_mid = layer_stats(middle)
    second_rows = normed_mid.astype(jnp.bfloat16)
    space_query = split_heads(project(second_rows, spatial_query))
    space_key = split_heads(project(second_rows, spatial_key))
    space_value = split_heads(project(second_rows, spatial_value))
    space_keys, space_values = (
        lax.all_gather(space_key, "space", axis=2, tiled=True),
        lax.all_gather(space_value, "space", axis=2, tiled=True),
    )
    space_blend, space_logsum = attend(space_query, space_keys, space_values, SPATIAL)
    space_grad_mix = split_heads(project(grad_out, spatial_out.T))
    space_offset = offsets(space_grad_mix, space_blend, SPATIAL)
    space_shares, space_grad_scores = score_grads(
        space_query, space_keys, space_values, space_grad_mix, space_logsum, space_offset, SPATIAL
    )
    space_grad_query = query_grad(space_grad_scores, space_keys, SPATIAL)
    all_query, all_grad_mix = (
        lax.all_gather(space_query, "space", axis=2, tiled=True),
        lax.all_gather(space_grad_mix, "space", axis=2, tiled=True),
    )
    all_logsum, all_offset = (
        lax.all_gather(space_logsum, "space", axis=3, tiled=True),
        lax.all_gather(space_offset, "space", axis=3, tiled=True),
    )
    owned_shares, owned_grad_scores = score_grads(
        all_query, space_key, space_value, all_grad_mix, all_logsum, all_offset, SPATIAL
    )
    space_grad_key, space_grad_value = key_grads(
        owned_shares, owned_grad_scores, all_query, all_grad_mix, SPATIAL
    )
    grad_second = back_project(
        (space_grad_query, space_grad_key, space_grad_value),
        (spatial_query, spatial_key, spatial_value),
    )
    grad_mid = (
        grad_out.astype(jnp.float32)
        + norm_grad(normed_mid, inverse_mid, grad_second.astype(jnp.float32))
    ).astype(jnp.bfloat16)
    time_grad_mix = split_heads(project(grad_mid, temporal_out.T))
    time_offset = offsets(time_grad_mix, time_blend, TEMPORAL)
    time_shares, time_grad_scores = score_grads(
        time_query, time_keys, time_values, time_grad_mix, time_logsum, time_offset, TEMPORAL
    )
    time_grad_query = query_grad(time_grad_scores, time_keys, TEMPORAL)
    every_query, every_grad_mix = (
        lax.all_gather(time_query, "tm", axis=1, tiled=True),
        lax.all_gather(time_grad_mix, "tm", axis=1, tiled=True),
    )
    every_logsum, every_offset = (
        lax.all_gather(time_logsum, "tm", axis=3, tiled=True),
        lax.all_gather(time_offset, "tm", axis=3, tiled=True),
    )
    owned_shares, owned_grad_scores = score_grads(
        every_query, time_key, time_value, every_grad_mix, every_logsum, every_offset, TEMPORAL
    )
    time_grad_key, time_grad_value = key_grads(
        owned_shares, owned_grad_scores, every_query, every_grad_mix, TEMPORAL
    )
    grad_first = back_project(
        (time_grad_query, time_grad_key, time_grad_value),
        (temporal_query, temporal_key, temporal_value),
    )
    return (
        grad_mid.astype(jnp.float32)
        + norm_grad(normed_in, inverse_in, grad_first.astype(jnp.float32))
    ).astype(jnp.bfloat16)


def solution(mesh):
    in_specs = (
        P(None, "tm", "space", None),
        P(None, "tm", "space", None),
        P(),
        P(),
        P(),
        P(),
        P(),
        P(),
        P(),
        P(),
    )
    out_specs = P(None, "tm", "space", None)
    return jax.shard_map(
        on_device, mesh=mesh, in_specs=in_specs, out_specs=out_specs, check_vma=False
    )
```

profile of v0, /device:TPU:1, one launch (start us, length us, event | category | flops | bytes accessed | tf_op | source)
XLA Modules:
  0.0 658.9 jit_solution(9733783031476466118)
XLA Ops:
  24.2 57.4 %all-gather.15.cloned.1.call-done = bf16[1,32,128,6,128]{4,2,3,0,1:T(8,128)(2,1)} async-done(((bf16[1,2,128,6,128]{4,2,3,0,1:T(8,128)(2,1)}), bf16[1,32,128,6,128]{4,2,3,0,1:T(8,128)(2,1)}) %all-gather.15.cloned.1.call-update) | async-done | bytes 6291472 | tf_op jit(solution)/shard_map/all_gather | solution.py:114
  81.6 24.6 %fusion.236 = (f32[128,6,2]{2,1,0:T(8,128)S(1)}, f32[128,6,2,32]{3,2,1,0:T(2,128)S(1)}) fusion(bf16[1,32,128,6,128]{4,2,3,0,1:T(8,128)(2,1)} %all-gather.15.cloned.1.call-done, bf16[2,128,6,128]{3,2,1,0:T(8,128)(2,1)} %reshape.469), kind=kOutput, calls=%fused_computation.176 | convolution fusion | flops 12679680 | bytes 6887424 | tf_op jit(solution)/shard_map/blghe,bmghe->bghlm/dot_general | solution.py:52
  109.9 35.7 %all-gather.13.cloned.1.call-done = bf16[1,32,128,6,128]{4,2,3,0,1:T(8,128)(2,1)} async-done(((bf16[1,2,128,6,128]{4,2,3,0,1:T(8,128)(2,1)}), bf16[1,32,128,6,128]{4,2,3,0,1:T(8,128)(2,1)}) %all-gather.13.cloned.1.call-update) | async-done | bytes 6291472 | tf_op jit(solution)/shard_map/all_gather | solution.py:115
  145.6 10.3 %fusion.88 = bf16[128,6,128,2]{2,3,1,0:T(2,128)(2,1)} fusion(bf16[1,32,128,6,128]{4,2,3,0,1:T(8,128)(2,1)} %all-gather.13.cloned.1.call-done, f32[128,6,2,32]{3,2,1,0:T(2,128)} %copy-done.17, f32[128,6,2]{2,1,0:T(8,128)} %log_add_fusion), kind=kOutput, calls=%fused_computation.87 | convolution fusion | flops 12877824 | bytes 6887424 | tf_op jit(solution)/shard_map/bghlm,bmghe->blghe/dot_general | solution.py:52
  183.4 3.5 convolution_convert_fusion.3
  207.9 27.7 %all-gather.17.cloned.1.call-done = bf16[1,2,1024,6,128]{4,2,3,1,0:T(8,128)(2,1)} async-done(((bf16[1,2,128,6,128]{4,2,3,1,0:T(8,128)(2,1)}), bf16[1,2,1024,6,128]{4,2,3,1,0:T(8,128)(2,1)}) %all-gather.17.cloned.1.call-update) | async-done | bytes 3145744 | tf_op jit(solution)/shard_map/all_gather | solution.py:126
  241.4 67.0 %all-gather.19.cloned.1.call-done = bf16[1,2,1024,6,128]{4,2,3,1,0:T(8,128)(2,1)} async-done(((bf16[1,2,128,6,128]{4,2,3,1,0:T(8,128)(2,1)}), bf16[1,2,1024,6,128]{4,2,3,1,0:T(8,128)(2,1)}) %all-gather.19.cloned.1.call-update) | async-done | bytes 3145744 | tf_op jit(solution)/shard_map/all_gather | solution.py:127
  308.4 5.7 fusion.176
  314.0 8.6 %fusion.171 = bf16[1,2,128,6,128]{2,4,3,1,0:T(8,128)(2,1)} fusion(f32[2,6,128,1024]{3,2,1,0:T(8,128)} %copy-done.2, f32[2,6,128]{2,1,0:T(8,128)S(1)} %fusion.176, f32[2,6,128]{2,1,0:T(8,128)S(1)} %log_add_fusion.1, bf16[1,2,1024,6,128]{4,2,3,1,0:T(8,128)(2,1)} %all-gather.19.cloned.1.call-done, ...), kind=kOutput, calls=%fused_computation.118 | convolution fusion | flops 814940160 | bytes 13381632 | tf_op jit(solution)/shard_map/bghlm,bgmhe->bglhe/dot_general | solution.py:52
  324.8 25.9 %all-gather.1 = f32[2,6,1024]{2,1,0:T(8,128)} all-gather(f32[2,6,128]{2,1,0:T(8,128)S(1)} %fusion.176), channel_id=3, replica_groups=mesh['tm'=16,'space'=8] {'space'}, dimensions={2}, use_global_device_ids=true | all-gather | bytes 55296 | tf_op jit(solution)/shard_map/all_gather | solution.py:142
  350.7 25.1 %all-gather = f32[2,6,1024]{2,1,0:T(8,128)} all-gather(f32[2,6,128]{2,1,0:T(8,128)S(1)} %log_add_fusion.1), channel_id=2, replica_groups=mesh['tm'=16,'space'=8] {'space'}, dimensions={2}, use_global_device_ids=true | all-gather | bytes 55296 | tf_op jit(solution)/shard_map/all_gather | solution.py:141
  375.8 7.1 %all-gather.21.cloned.1.call-done = bf16[1,2,1024,6,128]{4,2,3,1,0:T(8,128)(2,1)} async-done(((bf16[1,2,128,6,128]{4,2,3,1,0:T(8,128)(2,1)}), bf16[1,2,1024,6,128]{4,2,3,1,0:T(8,128)(2,1)}) %all-gather.21.cloned.1.call-update) | async-done | bytes 3145744 | tf_op jit(solution)/shard_map/all_gather | solution.py:137
  382.9 5.6 fusion.35
  388.5 67.4 %all-gather.23.cloned.1.call-done = bf16[1,2,1024,6,128]{4,2,3,1,0:T(8,128)(2,1)} async-done(((bf16[1,2,128,6,128]{4,2,3,1,0:T(8,128)(2,1)}), bf16[1,2,1024,6,128]{4,2,3,1,0:T(8,128)(2,1)}) %all-gather.23.cloned.1.call-update) | async-done | bytes 3145744 | tf_op jit(solution)/shard_map/all_gather | solution.py:138
  455.9 8.2 %fusion.166 = bf16[1,2,128,6,128]{2,4,3,1,0:T(8,128)(2,1)} fusion(f32[2,6,1024,128]{3,2,1,0:T(8,128)} %fusion.35, f32[2,6,1024]{2,1,0:T(8,128)} %all-gather.1, f32[2,6,1024]{2,1,0:T(8,128)} %all-gather, bf16[1,2,1024,6,128]{4,2,3,1,0:T(8,128)(2,1)} %all-gather.23.cloned.1.call-done, bf16[1,2,1024,6,128]{4,2,3,1,0:T(8,128)(2,1)} %all-gather.21.cloned.1.call-done, ...), kind=kOutput, calls=%fused_computation.117 | convolution fusion | flops 814940160 | bytes 13467648 | tf_op jit(solution)/shard_map/bghlm,bglhe->bgmhe/dot_general | solution.py:52
  465.5 5.7 fusion.137
  488.6 27.6 %all-gather.2 = f32[128,6,32]{0,1,2:T(8,128)S(1)} all-gather(f32[128,6,2]{0,1,2:T(8,128)S(1)} %copy.155), channel_id=4, replica_groups=mesh['tm'=16,'space'=8] {'tm'}, dimensions={2}, use_global_device_ids=true | all-gather | bytes 104448 | tf_op jit(solution)/shard_map/all_gather | solution.py:169
  517.3 7.6 %all-gather.25.cloned.1.call-done = bf16[1,32,128,6,128]{4,2,3,0,1:T(8,128)(2,1)} async-done(((bf16[1,2,128,6,128]{4,2,3,0,1:T(8,128)(2,1)}), bf16[1,32,128,6,128]{4,2,3,0,1:T(8,128)(2,1)}) %all-gather.25.cloned.1.call-update) | async-done | bytes 6291472 | tf_op jit(solution)/shard_map/all_gather | solution.py:165
  524.9 10.4 %fusion.116 = f32[128,6,32,2]{2,3,1,0:T(2,128)} fusion(bf16[1,32,128,6,128]{4,2,3,0,1:T(8,128)(2,1)} %all-gather.25.cloned.1.call-done, bf16[2,128,6,128]{3,2,1,0:T(8,128)(2,1)} %reshape.479, f32[128,6,32]{2,1,0:T(8,128)} %copy.156), kind=kOutput, calls=%fused_computation.103 | convolution fusion | flops 12681216 | bytes 6979584 | tf_op jit(solution)/shard_map/blghe,bmghe->bghlm/dot_general | solution.py:52
  545.9 28.8 %fusion.163 = bf16[1,2,128,6,128]{4,1,3,2,0:T(2,128)(2,1)} fusion(bf16[1,32,128,6,128]{4,2,3,0,1:T(8,128)(2,1)} %all-gather.15.cloned.1.call-done, bf16[2,128,6,128]{3,0,2,1:T(2,128)(2,1)S(1)} %copy-done.21, bf16[1,32,128,6,128]{4,2,3,0,1:T(8,128)(2,1)} %all-gather.13.cloned.1.call-done, f32[128,6,2,32]{3,2,1,0:T(2,128)} %copy-done.17, ...), kind=kOutput, calls=%fused_computation.116 | convolution fusion | flops 25608192 | bytes 13578240 | tf_op jit(solution)/shard_map/bghlm,bmghe->blghe/dot_general | solution.py:52
  576.1 21.9 %all-gather.3 = f32[128,6,32]{0,1,2:T(8,128)} all-gather(f32[128,6,2]{0,1,2:T(8,128)S(1)} %copy.181), channel_id=5, replica_groups=mesh['tm'=16,'space'=8] {'tm'}, dimensions={2}, use_global_device_ids=true | all-gather | bytes 104448 | tf_op jit(solution)/shard_map/all_gather | solution.py:170
  599.9 3.7 fusion.201
  603.6 28.1 %fusion.160 = bf16[1,2,128,6,128]{4,1,3,2,0:T(2,128)(2,1)} fusion(bf16[1,32,128,6,128]{4,2,3,0,1:T(8,128)(2,1)} %all-gather.25.cloned.1.call-done, f32[128,6,32,2]{2,3,1,0:T(2,128)} %fusion.116, bf16[1,32,128,6,128]{4,2,3,0,1:T(8,128)(2,1)} %all-gather.27.cloned.1.call-done, bf16[2,128,6,128]{3,2,1,0:T(8,128)(2,1)} %reshape.481, f32[128,6,32]{2,1,0:T(8,128)} %copy.162), kind=kOutput, calls=%fused_computation.115 | convolution fusion | flops 25559040 | bytes 13664256 | tf_op jit(solution)/shard_map/bghlm,blghe->bmghe/dot_general | solution.py:52
  633.1 9.9 %fusion.157 = bf16[1,2,128,6,128]{4,1,3,2,0:T(2,128)(2,1)} fusion(bf16[1,32,128,6,128]{4,2,3,0,1:T(8,128)(2,1)} %all-gather.27.cloned.1.call-done, f32[128,6,32,2]{2,3,1,0:T(2,128)} %fusion.116), kind=kOutput, calls=%fused_computation.114 | convolution fusion | flops 12828672 | bytes 6881280 | tf_op jit(solution)/shard_map/bghlm,blghe->bmghe/dot_general | solution.py:52
  (155 shorter events, 121.0 us)
Async XLA Ops:
  6.5 162.0 %copy-start = (bf16[1536,768]{1,0:T(8,128)(2,1)S(1)}, bf16[1536,768]{1,0:T(8,128)(2,1)}, u32[]{:S(2)}) copy-start(bf16[1536,768]{1,0:T(8,128)(2,1)} %param.18) | copy-start | bytes 7077892
  6.5 75.1 %all-gather.15.cloned.1.call-start = ((), (), s32[]{:S(2)}) async-start(), calls=%async_computation.1 | async-start | bytes 6684672 | tf_op jit(solution)/shard_map/all_gather | solution.py:114
  6.5 5.4 copy-start.12
  8.0 3.0 copy-start.22
  9.6 1.5 copy-start.26
  14.0 131.6 %all-gather.13.cloned.1.call-start = ((), (), s32[]{:S(2)}) async-start(), calls=%async_computation | async-start | bytes 6684672 | tf_op jit(solution)/shard_map/all_gather | solution.py:115
  19.8 215.9 %all-gather.17.cloned.1.call-start = ((), (), s32[]{:S(2)}) async-start(), calls=%async_computation.2 | async-start | bytes 3538944 | tf_op jit(solution)/shard_map/all_gather | solution.py:126
  22.9 1.3 copy-start.13
  156.0 4.8 copy-start.1
  161.0 1.7 copy-start.10
  168.4 139.9 %all-gather.19.cloned.1.call-start = ((), (), s32[]{:S(2)}) async-start(), calls=%async_computation.3 | async-start | bytes 3538944 | tf_op jit(solution)/shard_map/all_gather | solution.py:127
  175.3 207.6 %all-gather.21.cloned.1.call-start = ((), (), s32[]{:S(2)}) async-start(), calls=%async_computation.4 | async-start | bytes 3538944 | tf_op jit(solution)/shard_map/all_gather | solution.py:137
  183.3 272.6 %all-gather.23.cloned.1.call-start = ((), (), s32[]{:S(2)}) async-start(), calls=%async_computation.5 | async-start | bytes 3538944 | tf_op jit(solution)/shard_map/all_gather | solution.py:138
  191.0 333.9 %all-gather.25.cloned.1.call-start = ((), (), s32[]{:S(2)}) async-start(), calls=%async_computation.6 | async-start | bytes 6684672 | tf_op jit(solution)/shard_map/all_gather | solution.py:165
  195.2 408.4 %all-gather.27.cloned.1.call-start = ((), (), s32[]{:S(2)}) async-start(), calls=%async_computation.7 | async-start | bytes 6684672 | tf_op jit(solution)/shard_map/all_gather | solution.py:166
  238.8 2.6 copy-start.2
  465.5 6.2 copy-start.8
  465.5 6.2 copy-start.14
  471.7 1.7 copy-start.11
  476.4 1.7 copy-start.9
  517.3 18.0 %copy-start.15 = (bf16[256,768]{1,0:T(8,128)(2,1)S(1)}, bf16[256,768]{1,0:T(8,128)(2,1)}, u32[]{:S(2)}) copy-start(bf16[256,768]{1,0:T(8,128)(2,1)} %convolution_convert_fusion.1) | copy-start | bytes 1179652
  539.5 6.3 copy-start.21
  645.1 3.1 copy-start.7
  645.1 3.1 copy-start.16
  (14 other events, 13.7 us)
Sparse Core Ops, SparseCore 0:
  14.1 67.4 all-gather.14
  84.1 61.5 all-gather.12
  168.6 67.0 all-gather.16
  237.2 71.1 all-gather.18
  309.9 73.0 all-gather.20
  384.4 71.4 all-gather.22
  458.4 66.4 all-gather.24
  527.3 61.8 all-gather.26
where the time goes:
time: 664 us; the launch traced here: 659 us
  waiting for transfers between devices  270 us (41%)
  matrix products  182 us (27%)
  blocking collectives  101 us (15%)
  local copies, waits for them, and re-layouts  72.4 us (11%)
  other arithmetic  19 us (3%)
  between operations  14.2 us (2%)
    dot_general x12, matrix products, product(): jnp.einsum(einsum_form, left, right, preferred_element_type=jnp.float32)  149 us
    all_gather x1, waiting for transfers between devices, on_device(): lax.all_gather(space_grad_mix, 'space', axis=2, tiled=True)  67.4 us
    all_gather x1, waiting for transfers between devices, on_device(): lax.all_gather(space_value, 'space', axis=2, tiled=True)  67 us
    all_gather x1, waiting for transfers between devices, on_device(): lax.all_gather(time_key, 'tm', axis=1, tiled=True)  57.4 us
    all_gather x1, waiting for transfers between devices, on_device(): lax.all_gather(time_value, 'tm', axis=1, tiled=True)  35.7 us
    another operation x16, local copies, waits for them, and re-layouts, split_heads(): return values.reshape(values.shape[:-1] + (HEADS, HD))  28.2 us
    all_gather x1, waiting for transfers between devices, on_device(): lax.all_gather(space_key, 'space', axis=2, tiled=True)  27.7 us
    all_gather x1, blocking collectives, on_device(): lax.all_gather(time_logsum, 'tm', axis=3, tiled=True)  27.6 us
  transfers between devices with their start and end apart: 8, of which 7 were waited for; matrix products, arithmetic and copies ran while one was open for 29% of the time, Pallas kernels for 0%

commit v1 on v0

v1 whole, which is shorter than its diff:
```python
import jax
import jax.numpy as jnp
from jax import lax
from jax.sharding import PartitionSpec as P

HEADS = 6
HD = 128
SLOTS = 8
EPSILON = 1e-05
SCALE = HD ** (-0.5)
BF = jnp.bfloat16
F32 = jnp.float32


def layer_stats(values):
    centre = jnp.mean(values, axis=-1, keepdims=True)
    spread = jnp.mean(jnp.square(values - centre), axis=-1, keepdims=True)
    inverse = lax.rsqrt(spread + EPSILON)
    return ((values - centre) * inverse, inverse)


def norm_grad(normed, inverse, upstream):
    first_mean = jnp.mean(upstream, axis=-1, keepdims=True)
    cross_mean = jnp.mean(upstream * normed, axis=-1, keepdims=True)
    return inverse * (upstream - first_mean - normed * cross_mean)


def mm(left, right):
    return jnp.dot(left, right, preferred_element_type=F32)


def mmt(left, right):
    return lax.dot_general(left, right, (((1,), (1,)), ((), ())), preferred_element_type=F32)


def ein(form, left, right):
    return jnp.einsum(form, left, right, preferred_element_type=F32)


def forward(query, key, value, mask):
    scores = ein("glx,gmx->glm", query, key) * SCALE
    if mask is not None:
        scores = jnp.where(mask, scores, -jnp.inf)
    top = jnp.max(scores, axis=-1, keepdims=True)
    grown = jnp.exp(scores - top)
    shares = grown / jnp.sum(grown, axis=-1, keepdims=True)
    blend = ein("glm,gmx->glx", shares.astype(BF), value).astype(BF)
    return shares, blend


def backward(query, key, value, shares, blend, mix):
    offset = jnp.sum(mix.astype(F32) * blend.astype(F32), axis=-1, keepdims=True)
    grad_scores = (shares * (ein("glx,gmx->glm", mix, value) - offset) * SCALE).astype(BF)
    grad_query = ein("glm,gmx->glx", grad_scores, key).astype(BF)
    grad_key = ein("glm,glx->gmx", grad_scores, query).astype(BF)
    grad_value = ein("glm,glx->gmx", shares.astype(BF), mix).astype(BF)
    return grad_query, grad_key, grad_value


def to_time(rows):
    width = rows.shape[-1]
    moved = lax.all_to_all(rows.reshape(2, 128, width), "tm", 1, 0, tiled=True)
    return moved.reshape(256, width)


def to_home(rows):
    width = rows.shape[-1]
    moved = lax.all_to_all(rows.reshape(32, 8, width), "tm", 0, 1, tiled=True)
    return moved.reshape(256, width)


def heads_first(rows):
    return rows.reshape(256, HEADS, HD).transpose(1, 0, 2)


def heads_last(heads):
    return heads.transpose(1, 0, 2).reshape(256, HEADS * HD)


def to_heads(members):
    stacked = jnp.stack([heads_first(m) for m in members], axis=1)
    padded = jnp.pad(stacked, ((0, SLOTS - HEADS), (0, 0), (0, 0), (0, 0)))
    moved = lax.all_to_all(padded, "space", 0, 0, tiled=True)
    moved = moved.reshape(8, len(members), 2, 128, HD).transpose(1, 2, 0, 3, 4)
    return moved.reshape(len(members), 2, 1024, HD)


def from_heads(members):
    count = len(members)
    stacked = jnp.stack(members, axis=0).reshape(count, 2, 8, 128, HD).transpose(2, 0, 1, 3, 4)
    moved = lax.all_to_all(stacked, "space", 0, 0, tiled=True)
    kept = moved[:HEADS].reshape(HEADS, count, 256, HD)
    return [heads_last(kept[:, i]) for i in range(count)]


def on_device(tokens, grad_out, tq, tk, tv, to, sq, sk, sv, so):
    tokens = tokens.reshape(256, 1536)
    grad_out = grad_out.reshape(256, 1536)
    space_mix = mmt(grad_out, so).astype(BF)
    source = to_time(tokens).astype(F32)
    first_rows = layer_stats(source)[0].astype(BF)
    query, key, value = (heads_first(mm(first_rows, w).astype(BF)) for w in (tq, tk, tv))
    place = jnp.arange(256) % 8
    mask = (place[:, None] == place[None, :])[None]
    shares, blend = forward(query, key, value, mask)
    home_blend = to_home(heads_last(blend))
    branch = mm(home_blend, to).astype(BF)
    middle = tokens.astype(F32) + branch.astype(F32)
    normed_mid, inverse_mid = layer_stats(middle)
    second_rows = normed_mid.astype(BF)
    members = [mm(second_rows, w).astype(BF) for w in (sq, sk, sv)] + [space_mix]
    squery, skey, svalue, smix = to_heads(members)
    sshares, sblend = forward(squery, skey, svalue, None)
    grads = from_heads(backward(squery, skey, svalue, sshares, sblend, smix))
    grad_second = sum(mmt(g, w) for g, w in zip(grads, (sq, sk, sv))).astype(BF)
    grad_mid = (
        grad_out.astype(F32) + norm_grad(normed_mid, inverse_mid, grad_second.astype(F32))
    ).astype(BF)
    mix = heads_first(to_time(mmt(grad_mid, to).astype(BF)))
    tgrads = [heads_last(g) for g in backward(query, key, value, shares, blend, mix)]
    grad_first = to_home(sum(mmt(g, w) for g, w in zip(tgrads, (tq, tk, tv))).astype(BF))
    normed_in, inverse_in = layer_stats(tokens.astype(F32))
    grad_in = grad_mid.astype(F32) + norm_grad(normed_in, inverse_in, grad_first.astype(F32))
    return grad_in.astype(BF).reshape(1, 2, 128, 1536)


def solution(mesh):
    row = P(None, "tm", "space", None)
    return jax.shard_map(
        on_device,
        mesh=mesh,
        in_specs=(row, row) + (P(),) * 8,
        out_specs=row,
        check_vma=False,
    )
```

time: 664 us -> 251 us (0.38)
  waiting for transfers between devices: 270 us -> 31.9 us
  matrix products: 182 us -> 57.7 us
  blocking collectives: 101 us -> 68.6 us
  local copies, waits for them, and re-layouts: 72.4 us -> 51.6 us
  starting transfers between devices: 1.08 us -> 19.9 us
  between operations: 14.2 us -> 0.51 us
    all_gather x8 -> x0, waiting for transfers between devices: 270 us -> none  [the longest x1 67.4 us: on_device(): lax.all_gather(space_grad_mix, 'space', axis=2, tiled=True)]
    dot_general x27 -> x25, matrix products: 182 us -> 47.8 us  [the longest x7 19 us: mm(): return jnp.dot(left, right, preferred_element_type=F32)]
    all_gather x4 -> x0, blocking collectives: 101 us -> none  [the longest x1 27.6 us: on_device(): lax.all_gather(time_logsum, 'tm', axis=3, tiled=True)]
    all_to_all x0 -> x3, blocking collectives: none -> 68.6 us  [the longest x1 29.2 us: to_heads(): moved = lax.all_to_all(padded, 'space', 0, 0, tiled=True)]
    another operation x25 -> x4, local copies, waits for them, and re-layouts: 43.8 us -> 8.37 us  [the longest x2 4.26 us: heads_first(): return rows.reshape(256, HEADS, HD).transpose(1, 0, 2)]
    all_to_all x0 -> x3, waiting for transfers between devices: none -> 31.9 us  [the longest x2 18.6 us: to_home(): moved = lax.all_to_all(rows.reshape(32, 8, width), 'tm', 0, 1, tiled=True)]
    all_to_all x0 -> x3, starting transfers between devices: none -> 19.9 us  [the longest x2 10.5 us: to_home(): moved = lax.all_to_all(rows.reshape(32, 8, width), 'tm', 0, 1, tiled=True)]
    reshape x0 -> x3, local copies, waits for them, and re-layouts: none -> 10.5 us  [the longest x2 10.1 us: to_heads(): moved = moved.reshape(8, len(members), 2, 128, HD).transpose(1, 2, 0, 3, 4)]
  transfers between devices with their start and end apart: 8 -> 3, of which waited for: 7 -> 3; matrix products, arithmetic and copies ran while one was open for 29% -> 2% of each run, Pallas kernels for 0% -> 0%
where the time goes in v1:
time: 251 us; the launch traced here: 249 us
  blocking collectives  68.6 us (27%)
  matrix products  57.7 us (23%)
  local copies, waits for them, and re-layouts  51.6 us (21%)
  waiting for transfers between devices  31.9 us (13%)
  starting transfers between devices  19.9 us (8%)
  other arithmetic  18.6 us (7%)
    all_to_all x1, blocking collectives, to_heads(): moved = lax.all_to_all(padded, 'space', 0, 0, tiled=True)  29.2 us
    all_to_all x1, blocking collectives, from_heads(): moved = lax.all_to_all(stacked, 'space', 0, 0, tiled=True)  20.8 us
    dot_general x7, matrix products, mm(): return jnp.dot(left, right, preferred_element_type=F32)  19 us
    all_to_all x2, waiting for transfers between devices, to_home(): moved = lax.all_to_all(rows.reshape(32, 8, width), 'tm', 0, 1, tiled=True)  18.6 us
    all_to_all x1, blocking collectives, to_time(): moved = lax.all_to_all(rows.reshape(2, 128, width), 'tm', 1, 0, tiled=True)  18.6 us
    dot_general x8, matrix products, mmt(): lax.dot_general(left, right, (((1,), (1,)), ((), ())), preferred_element_...  15.8 us
    all_to_all x1, waiting for transfers between devices, to_time(): moved = lax.all_to_all(rows.reshape(2, 128, width), 'tm', 1, 0, tiled=True)  13.2 us
    dot_general x10, matrix products, ein(): return jnp.einsum(form, left, right, preferred_element_type=F32)  13 us
  transfers between devices with their start and end apart: 3, of which 3 were waited for; matrix products, arithmetic and copies ran while one was open for 2% of the time, Pallas kernels for 0%

profile of v1, /device:TPU:1, one launch (start us, length us, event | category | flops | bytes accessed | tf_op | source)
XLA Modules:
  0.0 248.7 jit_solution(18076176460510015678)
XLA Ops:
  0.0 3.0 %copy.232 = bf16[1,2,128,1536]{3,1,2,0:T(2,128)(2,1)} copy(bf16[1,2,128,1536]{3,2,1,0:T(8,128)(2,1)} %param.10) | data formatting | bytes 1572864 | tf_op args[0]
  3.0 9.4 %all-to-all-start = ((bf16[2,128,1536]{2,0,1:T(2,128)(2,1)}), bf16[2,128,1536]{2,0,1:T(2,128)(2,1)S(1)}, u32[]{:S(2)}, u32[]{:S(2)}) async-start(bf16[2,128,1536]{2,0,1:T(2,128)(2,1)} %bitcast.201), calls=%async_computation | async-start | bytes 1572864 | tf_op jit(solution)/shard_map/all_to_all | solution.py:62
  13.2 13.2 %all-to-all-done = bf16[2,128,1536]{2,0,1:T(2,128)(2,1)S(1)} async-done(((bf16[2,128,1536]{2,0,1:T(2,128)(2,1)}), bf16[2,128,1536]{2,0,1:T(2,128)(2,1)S(1)}, u32[]{:S(2)}, u32[]{:S(2)}) %all-to-all-start) | async-done | bytes 786464 | tf_op jit(solution)/shard_map/all_to_all | solution.py:62
  33.8 3.3 %convolution_convert_fusion.14 = bf16[256,768]{1,0:T(8,128)(2,1)} fusion(bf16[256,1536]{1,0:T(8,128)(2,1)S(1)} %fusion.19, bf16[1536,768]{1,0:T(8,128)(2,1)} %param.14), kind=kOutput, calls=%fused_computation.69 | convolution fusion | flops 604176384 | bytes 3538944 | tf_op jit(solution)/shard_map/dot_general | solution.py:29
  39.1 3.2 %convolution_convert_fusion.16 = bf16[256,768]{1,0:T(8,128)(2,1)} fusion(bf16[256,1536]{1,0:T(8,128)(2,1)S(1)} %fusion.19, bf16[1536,768]{1,0:T(8,128)(2,1)} %param.12), kind=kOutput, calls=%fused_computation.71 | convolution fusion | flops 604176384 | bytes 3538944 | tf_op jit(solution)/shard_map/dot_general | solution.py:29
  43.5 2.8 %fusion.49 = (f32[6,256]{1,0:T(8,128)S(1)}, f32[6,256,256]{1,2,0:T(8,128)}) fusion(bf16[6,256,128]{1,2,0:T(8,128)(2,1)S(1)} %bitcast.226, bf16[6,256,128]{1,2,0:T(8,128)(2,1)S(1)} %bitcast.224, pred[256,256]{0,1:T(8,128)(4,1)} %broadcast_compare_fusion), kind=kOutput, calls=%fused_computation.107 | convolution fusion | flops 102236416 | bytes 2430976 | tf_op jit(solution)/shard_map/sub | solution.py:45
  49.7 5.2 %all-to-all-start.1 = ((bf16[32,8,768]{2,1,0:T(8,128)(2,1)}), bf16[32,8,768]{2,1,0:T(8,128)(2,1)}, u32[]{:S(2)}, u32[]{:S(2)}) async-start(bf16[32,8,768]{2,1,0:T(8,128)(2,1)} %reshape_reshape.10), calls=%async_computation.1 | async-start | bytes 786432 | tf_op jit(solution)/shard_map/all_to_all | solution.py:68
  54.9 3.5 %convolution_convert_fusion.10 = bf16[256,768]{1,0:T(8,128)(2,1)} fusion(bf16[256,1536]{1,0:T(8,128)(2,1)} %bitcast.229, bf16[768,1536]{1,0:T(8,128)(2,1)} %param.19), kind=kOutput, calls=%fused_computation.65 | convolution fusion | flops 604176384 | bytes 3538944 | tf_op jit(solution)/shard_map/dot_general | solution.py:33
  59.7 5.2 %all-to-all-done.1 = bf16[32,8,768]{2,1,0:T(8,128)(2,1)} async-done(((bf16[32,8,768]{2,1,0:T(8,128)(2,1)}), bf16[32,8,768]{2,1,0:T(8,128)(2,1)}, u32[]{:S(2)}, u32[]{:S(2)}) %all-to-all-start.1) | async-done | bytes 393248 | tf_op jit(solution)/shard_map/all_to_all | solution.py:68
  73.9 3.4 %convolution_convert_fusion.12 = bf16[256,768]{1,0:T(8,128)(2,1)} fusion(bf16[256,1536]{1,0:T(8,128)(2,1)} %copy-done.21, bf16[1536,768]{1,0:T(8,128)(2,1)} %param.17), kind=kOutput, calls=%fused_computation.67 | convolution fusion | flops 604176384 | bytes 3538944 | tf_op jit(solution)/shard_map/dot_general | solution.py:29
  79.3 3.4 %convolution_convert_fusion.13 = bf16[256,768]{1,0:T(8,128)(2,1)} fusion(bf16[256,1536]{1,0:T(8,128)(2,1)} %copy-done.21, bf16[1536,768]{1,0:T(8,128)(2,1)} %param.16), kind=kOutput, calls=%fused_computation.68 | convolution fusion | flops 604176384 | bytes 3538944 | tf_op jit(solution)/shard_map/dot_general | solution.py:29
  86.5 29.2 %all_to_all.58 = bf16[8,4,256,128]{2,3,1,0:T(8,128)(2,1)} all-to-all(bf16[8,4,256,128]{2,3,1,0:T(8,128)(2,1)S(1)} %pad.4.clone), channel_id=1, replica_groups=mesh['tm'=16,'space'=8] {'space'}, dimensions={0} | all-to-all | bytes 4194304 | tf_op jit(solution)/shard_map/all_to_all | solution.py:83
  115.6 4.0 %reshape.285 = bf16[8,4,2,128,128]{3,2,4,1,0:T(2,128)(2,1)} reshape(bf16[8,4,256,128]{2,3,1,0:T(8,128)(2,1)} %all_to_all.58) | data formatting | bytes 4194304 | tf_op jit(solution)/shard_map/reshape | solution.py:84
  119.6 6.1 %copy.169 = bf16[8,4,2,128,128]{4,3,0,2,1:T(8,128)(2,1)} copy(bf16[8,4,2,128,128]{3,2,4,1,0:T(2,128)(2,1)} %reshape.285) | data formatting | bytes 4194304 | tf_op jit(solution)/shard_map/reshape | solution.py:84
  125.8 2.9 %fusion.48 = (bf16[1,2,8,128,128]{4,3,2,1,0:T(8,128)(2,1)}, bf16[1,2,8,128,128]{4,3,2,1,0:T(8,128)(2,1)}, bf16[1,2,8,128,128]{4,3,2,1,0:T(8,128)(2,1)}, bf16[1,2,8,128,128]{4,3,2,1,0:T(8,128)(2,1)}) fusion(bf16[4,2,8,128,128]{4,3,2,1,0:T(8,128)(2,1)} %bitcast.199), kind=kLoop, calls=%fused_computation.106 | loop fusion | bytes 4194304 | tf_op jit(solution)/shard_map/unstack | solution.py:112
  128.7 7.1 %fusion.51 = (f32[2,1024]{1,0:T(2,128)S(1)}, f32[2,1024,1024]{1,2,0:T(8,128)}) fusion(bf16[2,1024,128]{2,1,0:T(8,128)(2,1)} %bitcast.208, bf16[2,1024,128]{2,1,0:T(8,128)(2,1)} %bitcast.206), kind=kOutput, calls=%fused_computation.109 | convolution fusion | flops 543163392 | bytes 9445376 | tf_op jit(solution)/shard_map/sub | solution.py:45
  135.8 4.7 %fusion.6 = bf16[2,1024,1024]{1,2,0:T(8,128)(2,1)S(1)} fusion(f32[2,1024,1024]{1,2,0:T(8,128)} %get-tuple-element.25, f32[2,1024]{1,0:T(2,128)S(1)} %get-tuple-element.24), kind=kLoop, calls=%fused_computation.8 | loop fusion | flops 4194304 | bytes 12591104 | tf_op jit(solution)/shard_map/convert_element_type | solution.py:47
  148.8 20.8 %all_to_all.59 = bf16[8,3,2,128,128]{4,3,2,1,0:T(8,128)(2,1)S(1)} all-to-all(bf16[8,3,2,128,128]{4,3,2,1,0:T(8,128)(2,1)S(1)} %copy_bitcast_fusion), channel_id=1, replica_groups=mesh['tm'=16,'space'=8] {'space'}, dimensions={0} | all-to-all | bytes 3145728 | tf_op jit(solution)/shard_map/all_to_all | solution.py:91
  172.6 3.8 %fusion.52 = f32[256,1536]{1,0:T(8,128)} fusion(bf16[256,768]{0,1:T(8,128)(2,1)} %bitcast.222, bf16[1536,768]{1,0:T(8,128)(2,1)} %param.16), kind=kOutput, calls=%fused_computation.110 | convolution fusion | flops 603979776 | bytes 4325376 | tf_op jit(solution)/shard_map/dot_general | solution.py:33
  178.5 3.2 %convolution_add_fusion.3 = f32[256,1536]{1,0:T(8,128)S(1)} fusion(f32[256,1536]{1,0:T(8,128)} %fusion.52, bf16[256,768]{0,1:T(8,128)(2,1)} %bitcast.220, bf16[1536,768]{1,0:T(8,128)(2,1)} %param.17), kind=kOutput, calls=%fused_computation.12 | convolution fusion | flops 604372992 | bytes 5898240 | tf_op jit(solution)/shard_map/dot_general | solution.py:33
  185.8 18.6 %all_to_all.60 = bf16[2,128,768]{2,0,1:T(2,128)(2,1)S(1)} all-to-all(bf16[2,128,768]{2,0,1:T(2,128)(2,1)S(1)} %copy.181), channel_id=1, replica_groups=mesh['tm'=16,'space'=8] {'tm'}, dimensions={1} | all-to-all | bytes 786432 | tf_op jit(solution)/shard_map/all_to_all | solution.py:62
  221.2 5.3 %all-to-all-start.5 = ((bf16[32,8,1536]{2,1,0:T(8,128)(2,1)}), bf16[32,8,1536]{2,1,0:T(8,128)(2,1)}, u32[]{:S(2)}, u32[]{:S(2)}) async-start(bf16[32,8,1536]{2,1,0:T(8,128)(2,1)} %fusion.12), calls=%async_computation.5 | async-start | bytes 1572864 | tf_op jit(solution)/shard_map/all_to_all | solution.py:68
  227.3 13.4 %all-to-all-done.5 = bf16[32,8,1536]{2,1,0:T(8,128)(2,1)} async-done(((bf16[32,8,1536]{2,1,0:T(8,128)(2,1)}), bf16[32,8,1536]{2,1,0:T(8,128)(2,1)}, u32[]{:S(2)}, u32[]{:S(2)}) %all-to-all-start.5) | async-done | bytes 786464 | tf_op jit(solution)/shard_map/all_to_all | solution.py:68
  245.6 3.1 %fusion.17 = bf16[256,1536]{1,0:T(8,128)(2,1)} fusion(f32[2,16,8,1536]{3,2,1,0:T(8,128)} %copy.191, bf16[1,2,128,1536]{3,2,1,0:T(8,128)(2,1)S(1)} %copy-done.3, bf16[256,1536]{1,0:T(8,128)(2,1)} %copy-done.5, f32[256]{0:T(256)S(1)} %div.74, f32[256]{0:T(256)S(1)} %get-tuple-element.18, f32[256]{0:T(256)S(1)} %div.70, f32[256]{0:T(256)S(1)} %get-tuple-element.16), kind=kLoop, calls=%fused_computation.28 | loop fusion | flops 3932160 | bytes 3936256 | tf_op jit(solution)/shard_map/convert_element_type | solution.py:124
  (134 shorter events, 70.2 us)
Async XLA Ops:
  0.0 70.5 %copy-start = (bf16[1536,768]{1,0:T(8,128)(2,1)S(1)}, bf16[1536,768]{1,0:T(8,128)(2,1)}, u32[]{:S(2)}) copy-start(bf16[1536,768]{1,0:T(8,128)(2,1)} %param.18) | copy-start | bytes 7077892
  3.0 23.4 %all-to-all-start = ((bf16[2,128,1536]{2,0,1:T(2,128)(2,1)}), bf16[2,128,1536]{2,0,1:T(2,128)(2,1)S(1)}, u32[]{:S(2)}, u32[]{:S(2)}) async-start(bf16[2,128,1536]{2,0,1:T(2,128)(2,1)} %bitcast.201), calls=%async_computation | async-start | bytes 1572864 | tf_op jit(solution)/shard_map/all_to_all | solution.py:62
  29.0 2.1 copy-start.9
  33.8 9.6 %copy-start.17 = (bf16[256,768]{0,1:T(8,128)(2,1)}, bf16[256,768]{0,1:T(8,128)(2,1)S(1)}, u32[]{:S(2)}) copy-start(bf16[256,768]{0,1:T(8,128)(2,1)S(1)} %copy.157) | copy-start | bytes 1179652
  43.5 2.9 %copy-start.19 = (bf16[256,768]{0,1:T(8,128)(2,1)}, bf16[256,768]{0,1:T(8,128)(2,1)S(1)}, u32[]{:S(2)}) copy-start(bf16[256,768]{0,1:T(8,128)(2,1)S(1)} %copy.156) | copy-start | bytes 1179652
  48.2 6.8 %copy-start.14 = (bf16[6,256,128]{1,2,0:T(8,128)(2,1)}, bf16[6,256,128]{1,2,0:T(8,128)(2,1)S(1)}, u32[]{:S(2)}) copy-start(bf16[6,256,128]{1,2,0:T(8,128)(2,1)S(1)} %convolution_convert_fusion.6) | copy-start | bytes 1179652
  49.7 15.2 %all-to-all-start.1 = ((bf16[32,8,768]{2,1,0:T(8,128)(2,1)}), bf16[32,8,768]{2,1,0:T(8,128)(2,1)}, u32[]{:S(2)}, u32[]{:S(2)}) async-start(bf16[32,8,768]{2,1,0:T(8,128)(2,1)} %reshape_reshape.10), calls=%async_computation.1 | async-start | bytes 786432 | tf_op jit(solution)/shard_map/all_to_all | solution.py:68
  58.4 7.5 %copy-start.3 = (bf16[1,2,128,1536]{3,2,1,0:T(8,128)(2,1)S(1)}, bf16[1,2,128,1536]{3,2,1,0:T(8,128)(2,1)}, u32[]{:S(2)}) copy-start(bf16[1,2,128,1536]{3,2,1,0:T(8,128)(2,1)} %param.10) | copy-start | bytes 2359300
  68.4 1.2 copy-start.1
  135.8 4.7 %copy-start.13 = (bf16[1,2,8,128,128]{4,3,2,1,0:T(8,128)(2,1)S(1)}, bf16[1,2,8,128,128]{4,3,2,1,0:T(8,128)(2,1)}, u32[]{:S(2)}) copy-start(bf16[1,2,8,128,128]{4,3,2,1,0:T(8,128)(2,1)} %get-tuple-element.10) | copy-start | bytes 1572868
  135.8 6.0 %copy-start.23 = (bf16[1,2,8,128,128]{4,3,2,1,0:T(8,128)(2,1)S(1)}, bf16[1,2,8,128,128]{4,3,2,1,0:T(8,128)(2,1)}, u32[]{:S(2)}) copy-start(bf16[1,2,8,128,128]{4,3,2,1,0:T(8,128)(2,1)} %get-tuple-element.9) | copy-start | bytes 1572868
  140.5 3.4 %copy-start.4 = (f32[2,1024,1024]{1,2,0:T(8,128)S(1)}, f32[2,1024,1024]{1,2,0:T(8,128)}, u32[]{:S(2)}) copy-start(f32[2,1024,1024]{1,2,0:T(8,128)} %get-tuple-element.25) | copy-start | bytes 25165828
  143.9 1.7 copy-start.12
  145.6 1.3 copy-start.11
  178.5 3.2 %copy-start.2 = (f32[256,1536]{1,0:T(8,128)S(1)}, f32[256,1536]{1,0:T(8,128)}, u32[]{:S(2)}) copy-start(f32[256,1536]{1,0:T(8,128)} %copy-done.1) | copy-start | bytes 4718596
  182.9 1.7 copy-start.8
  204.4 5.1 %copy-start.15 = (bf16[6,256,128]{1,2,0:T(8,128)(2,1)S(1)}, bf16[6,256,128]{1,2,0:T(8,128)(2,1)}, u32[]{:S(2)}) copy-start(bf16[6,256,128]{1,2,0:T(8,128)(2,1)} %copy-done.14) | copy-start | bytes 1179652
  210.6 2.2 copy-start.18
  212.9 1.4 copy-start.16
  212.9 1.6 copy-start.24
  214.5 1.7 copy-start.7
  216.2 1.7 copy-start.10
  217.8 1.7 copy-start.6
  221.2 19.5 %all-to-all-start.5 = ((bf16[32,8,1536]{2,1,0:T(8,128)(2,1)}), bf16[32,8,1536]{2,1,0:T(8,128)(2,1)}, u32[]{:S(2)}, u32[]{:S(2)}) async-start(bf16[32,8,1536]{2,1,0:T(8,128)(2,1)} %fusion.12), calls=%async_computation.5 | async-start | bytes 1572864 | tf_op jit(solution)/shard_map/all_to_all | solution.py:68
  (4 other events, 3.9 us)

commit v2 on v1

v2 whole, which is shorter than its diff:
```python
import math

import jax
import jax.numpy as jnp
from jax import lax
from jax.experimental import pallas as pl
from jax.experimental.pallas import tpu as pltpu
from jax.sharding import PartitionSpec as P

EPSILON = 1e-05
SCALE = 128 ** (-0.5)
SCALE2 = SCALE * math.log2(math.e)
BF = jnp.bfloat16
F32 = jnp.float32
D = 1536
HW = 768
MESH = pl.DeviceIdType.MESH


def mm(left, right):
    return jnp.dot(left, right, preferred_element_type=F32)


def mmt(left, right):
    return lax.dot_general(left, right, (((1,), (1,)), ((), ())), preferred_element_type=F32)


def tmm(left, right):
    return lax.dot_general(left, right, (((0,), (0,)), ((), ())), preferred_element_type=F32)


def mean(rows):
    return jnp.sum(rows, axis=-1, keepdims=True) * (1.0 / D)


def layer_stats(rows):
    centred = rows - mean(rows)
    inverse = lax.rsqrt(mean(centred * centred) + EPSILON)
    return centred * inverse, inverse


def norm_grad(normed, inverse, upstream):
    return inverse * (upstream - mean(upstream) - normed * mean(upstream * normed))


def rows16(ref, i):
    part = ref[i // 8, pl.ds((i % 8) * 2, 2)]
    return part.astype(F32).reshape(16, part.shape[-1])


def kernel(
    tok, gout, tq, tk, tv, to, sq, sk, sv, so,
    out,
    w_tq, w_tk, w_tv, w_to, w_sq, w_sk, w_sv, w_so,
    tok_h, gout_v, tok_t, nin, iin, rows_b, q_t, k_t, v_t, p_t, b_t,
    blend_s, blend_h, wide, nmid, imid,
    k_s, v_s, q_s, g_s, k_l, v_l, q_l, g_l,
    gq_a, gk_f, gv_f, gk_a, gv_a, gq_l, gk_l, gv_l,
    acc, gmid, mix_s, mix_l, tg, first_s, first_l,
    load_sem, tm_send, tm_recv, sp_send, sp_recv, back_send, back_recv,
):
    me_t = lax.axis_index("tm")
    me_s = lax.axis_index("space")

    loads = [
        pltpu.make_async_copy(src, dst, load_sem.at[n])
        for n, (src, dst) in enumerate((
            (gout, gout_v), (so, w_so), (tok, tok_h), (tq, w_tq), (tk, w_tk), (tv, w_tv),
            (to, w_to), (sk, w_sk), (sv, w_sv), (sq, w_sq),
        ))
    ]
    for load in loads:
        load.start()

    barrier = pltpu.get_barrier_semaphore()

    def greet_t(k, c):
        pl.semaphore_signal(barrier, 1, device_id={"tm": (me_t + k) % 16}, device_id_type=MESH)
        return c

    def greet_s(k, c):
        pl.semaphore_signal(barrier, 1, device_id={"space": (me_s + k) % 8}, device_id_type=MESH)
        return c

    lax.fori_loop(1, 16, greet_t, 0)
    lax.fori_loop(1, 8, greet_s, 0)
    pl.semaphore_wait(barrier, 22)

    def tm_copy(phase, src, dst, peer):
        return pltpu.make_async_remote_copy(
            src_ref=src, dst_ref=dst, send_sem=tm_send.at[phase, peer], recv_sem=tm_recv.at[phase, me_t],
            device_id={"tm": peer}, device_id_type=MESH)

    def time_part(ref, n):
        return ref.at[pl.ds(2 * n, 2)]

    def home_part(ref, n):
        return ref.at[:, n]

    def tm_start(phase, src, src_part, dst, dst_part):
        pltpu.make_async_copy(src_part(src, me_t), dst_part(dst, me_t), tm_recv.at[phase, me_t]).start()

        def go(k, c):
            peer = (me_t + k) % 16
            tm_copy(phase, src_part(src, peer), dst_part(dst, me_t), peer).start()
            return c

        lax.fori_loop(1, 16, go, 0)

    def tm_wait(phase, dst, dst_part):
        def go(n, c):
            part = dst_part(dst, n)
            pltpu.make_async_copy(part, part, tm_recv.at[phase, n]).wait()
            return c

        lax.fori_loop(0, 16, go, 0)

    def tm_sent(phase, src, src_part, dst, dst_part):
        def go(k, c):
            peer = (me_t + k) % 16
            tm_copy(phase, src_part(src, peer), dst_part(dst, me_t), peer).wait_send()
            return c

        lax.fori_loop(1, 16, go, 0)

    def slab(ref, n, whole, rows):
        if whole:
            return ref.at[n // 4, n % 4]
        half = 4 + (n % 4) // 2
        if rows == 128:
            return ref.at[n // 4, half]
        return ref.at[n // 4, half, pl.ds(pl.multiple_of((n % 2) * 64, 64), 64)]

    def stripe(ref, n, whole, rows):
        if len(ref.shape) == 3:
            return ref.at[0 if whole else 1, pl.ds(pl.multiple_of(n * 128, 128), 128)]
        if whole:
            return ref.at[pl.ds(pl.multiple_of(n * 128, 128), 128)]
        return ref.at[pl.ds(pl.multiple_of(1024 + n * 64, 64), 64)]

    def sp_copies(which, src, dst, peer, rows):
        return [
            pltpu.make_async_remote_copy(
                src_ref=slab(src, peer, whole, rows), dst_ref=stripe(dst, me_s, whole, rows),
                send_sem=sp_send.at[which, kind, peer], recv_sem=sp_recv.at[which, kind, me_s],
                device_id={"space": peer}, device_id_type=MESH)
            for kind, whole in enumerate((True, False))
        ]

    def sp_start(which, src, dst, rows):
        for kind, whole in enumerate((True, False)):
            pltpu.make_async_copy(
                slab(src, me_s, whole, rows), stripe(dst, me_s, whole, rows), sp_recv.at[which, kind, me_s]
            ).start()

        def go(k, c):
            for copy in sp_copies(which, src, dst, (me_s + k) % 8, rows):
                copy.start()
            return c

        lax.fori_loop(1, 8, go, 0)

    def sp_wait(which, dst, rows):
        def go(n, c):
            for kind, whole in enumerate((True, False)):
                part = stripe(dst, n, whole, rows)
                pltpu.make_async_copy(part, part, sp_recv.at[which, kind, n]).wait()
            return c

        lax.fori_loop(0, 8, go, 0)

    def sp_sent(which, src, dst, rows):
        def go(k, c):
            for copy in sp_copies(which, src, dst, (me_s + k) % 8, rows):
                copy.wait_send()
            return c

        lax.fori_loop(1, 8, go, 0)

    def home_slot(ref, n, whole, rows):
        if whole:
            return ref.at[n // 4, n % 4]
        if rows == 64:
            return ref.at[n // 4, 4 + (n % 4) // 2, pl.ds(pl.multiple_of((n % 2) * 64, 64), 64)]
        return ref.at[n // 4, 4 + n % 4]

    def back_copies(which, src, dst, peer, rows):
        return [
            pltpu.make_async_remote_copy(
                src_ref=stripe(src, peer, whole, rows), dst_ref=home_slot(dst, me_s, whole, rows),
                send_sem=back_send.at[which, kind, peer], recv_sem=back_recv.at[which, kind, me_s],
                device_id={"space": peer}, device_id_type=MESH)
            for kind, whole in enumerate((True, False))
        ]

    def back_start(which, src, dst, rows):
        for kind, whole in enumerate((True, False)):
            pltpu.make_async_copy(
                stripe(src, me_s, whole, rows), home_slot(dst, me_s, whole, rows), back_recv.at[which, kind, me_s]
            ).start()

        def go(k, c):
            for copy in back_copies(which, src, dst, (me_s + k) % 8, rows):
                copy.start()
            return c

        lax.fori_loop(1, 8, go, 0)

    def back_wait(which, dst, rows):
        def go(n, c):
            for kind, whole in enumerate((True, False)):
                part = home_slot(dst, n, whole, rows)
                pltpu.make_async_copy(part, part, back_recv.at[which, kind, n]).wait()
            return c

        lax.fori_loop(0, 8, go, 0)

    def back_sent(which, src, dst, rows):
        def go(k, c):
            for copy in back_copies(which, src, dst, (me_s + k) % 8, rows):
                copy.wait_send()
            return c

        lax.fori_loop(1, 8, go, 0)

    def put_heads(ref, flat):
        for t in range(2):
            for h in range(6):
                ref[t, h] = flat[t * 128:(t + 1) * 128, h * 128:(h + 1) * 128]

    tm_start(0, tok, home_part, tok_t, time_part)

    loads[0].wait()
    loads[1].wait()
    put_heads(g_s, mmt(gout_v[...], w_so[...]).astype(BF))
    sp_start(3, g_s, g_l, 64)

    loads[2].wait()

    def norm_home(i, c):
        normed, inverse = layer_stats(rows16(tok_h, i))
        at = pl.ds(pl.multiple_of(i * 16, 16), 16)
        nin[at] = normed
        iin[at] = inverse
        return c

    lax.fori_loop(0, 16, norm_home, 0)

    tm_wait(0, tok_t, time_part)

    def norm_time(i, c):
        normed, _ = layer_stats(tok_t[pl.ds(i * 2, 2)].astype(F32).reshape(16, D))
        rows_b[pl.ds(pl.multiple_of(i * 16, 16), 16)] = normed.astype(BF)
        return c

    lax.fori_loop(0, 16, norm_time, 0)
    for n, (weight, dst) in enumerate(((w_tq, q_t), (w_tk, k_t), (w_tv, v_t))):
        loads[3 + n].wait()
        flat = mm(rows_b[...], weight[...]).astype(BF)
        for h in range(6):
            dst[h] = flat[:, h * 128:(h + 1) * 128]

    patch_q = lax.broadcasted_iota(jnp.int32, (256, 256), 0) % 8
    patch_k = lax.broadcasted_iota(jnp.int32, (256, 256), 1) % 8
    same = patch_q == patch_k

    for h in range(6):
        scores = jnp.where(same, mmt(q_t[h], k_t[h]), -jnp.inf)
        grown = jnp.exp2((scores - jnp.max(scores, axis=-1, keepdims=True)) * SCALE2)
        shares = grown * (1.0 / jnp.sum(grown, axis=-1, keepdims=True))
        p_t[h] = shares
        blend = mm(shares.astype(BF), v_t[h])
        b_t[h] = blend.astype(BF)
        blend_s[:, :, h * 128:(h + 1) * 128] = blend.reshape(32, 8, 128).astype(BF)
    tm_start(1, blend_s, time_part, blend_h, home_part)

    loads[6].wait()
    tm_wait(1, blend_h, home_part)
    home = blend_h[...].astype(F32).reshape(256, HW).astype(BF)
    wide[...] = mm(home, w_to[...]).astype(BF)

    def norm_mid(i, c):
        at = pl.ds(pl.multiple_of(i * 16, 16), 16)
        normed, inverse = layer_stats(rows16(tok_h, i) + wide[at].astype(F32))
        nmid[at] = normed
        imid[at] = inverse
        rows_b[at] = normed.astype(BF)
        return c

    lax.fori_loop(0, 16, norm_mid, 0)
    for n, (weight, src, dst, rows) in enumerate((
        (w_sk, k_s, k_l, 128), (w_sv, v_s, v_l, 128), (w_sq, q_s, q_l, 64),
    )):
        loads[7 + n].wait()
        put_heads(src, mm(rows_b[...], weight[...]).astype(BF))
        sp_start(n, src, dst, rows)

    sp_wait(3, g_l, 64)
    sp_wait(0, k_l, 128)
    sp_wait(1, v_l, 128)
    sp_wait(2, q_l, 64)
    gk_f[...] = jnp.zeros_like(gk_f)
    gv_f[...] = jnp.zeros_like(gv_f)

    def attend(i, c):
        u = i // 4
        at = pl.ds(pl.multiple_of(i * 256, 256), 256)
        query, mix, key, value = q_l[at], g_l[at], k_l[u], v_l[u]
        scores = mmt(query, key)
        grown = jnp.exp2((scores - jnp.max(scores, axis=-1, keepdims=True)) * SCALE2)
        shares = grown * (1.0 / jnp.sum(grown, axis=-1, keepdims=True))
        rounded = shares.astype(BF)
        blend = mm(rounded, value).astype(BF)
        offset = jnp.sum(mix.astype(F32) * blend.astype(F32), axis=-1, keepdims=True)
        grads = (shares * (mmt(mix, value) - offset) * SCALE).astype(BF)
        gq_a[at] = mm(grads, key).astype(BF)
        gk_f[u] += tmm(grads, query)
        gv_f[u] += tmm(rounded, mix)
        return c

    lax.fori_loop(0, 6, attend, 0)
    back_start(0, gq_a, gq_l, 64)
    gk_a[...] = gk_f[...].astype(BF)
    back_start(1, gk_a, gk_l, 128)
    gv_a[...] = gv_f[...].astype(BF)
    back_start(2, gv_a, gv_l, 128)

    def take(ref, h):
        return ref[:, h].reshape(256, 128)

    def joined(ref):
        parts = [take(ref, h) for h in range(4)]
        for h in (4, 6):
            parts.append((take(ref, h).astype(F32) + take(ref, h + 1).astype(F32)).astype(BF))
        return jnp.concatenate(parts, axis=-1)

    back_wait(0, gq_l, 64)
    acc[...] = mmt(jnp.concatenate([take(gq_l, h) for h in range(6)], axis=-1), w_sq[...])
    back_wait(1, gk_l, 128)
    acc[...] += mmt(joined(gk_l), w_sk[...])
    back_wait(2, gv_l, 128)
    acc[...] += mmt(joined(gv_l), w_sv[...])

    def grad_norm_mid(i, c):
        at = pl.ds(pl.multiple_of(i * 16, 16), 16)
        upstream = acc[at].astype(BF).astype(F32)
        grad = norm_grad(nmid[at], imid[at], upstream)
        gmid[at] = (gout_v[at].astype(F32) + grad).astype(BF)
        return c

    lax.fori_loop(0, 16, grad_norm_mid, 0)
    mix_s[...] = mmt(gmid[...], w_to[...]).reshape(2, 16, 8, HW).astype(BF)
    tm_start(2, mix_s, home_part, mix_l, time_part)
    tm_wait(2, mix_l, time_part)

    for h in range(6):
        cols = pl.ds(h * 128, 128)
        mix = mix_l[:, :, cols].astype(F32).reshape(256, 128)
        offset = jnp.sum(mix * b_t[h].astype(F32), axis=-1, keepdims=True)
        mix = mix.astype(BF)
        shares = p_t[h]
        grads = (shares * (mmt(mix, v_t[h]) - offset) * SCALE).astype(BF)
        tg[0, :, cols] = mm(grads, k_t[h]).astype(BF)
        tg[1, :, cols] = tmm(grads, q_t[h]).astype(BF)
        tg[2, :, cols] = tmm(shares.astype(BF), mix).astype(BF)
    acc[...] = mmt(tg[0], w_tq[...])
    acc[...] += mmt(tg[1], w_tk[...])
    acc[...] += mmt(tg[2], w_tv[...])
    first_s[...] = acc[...].reshape(32, 8, D).astype(BF)
    tm_start(3, first_s, time_part, first_l, home_part)
    tm_wait(3, first_l, home_part)

    def grad_norm_in(i, c):
        at = pl.ds(pl.multiple_of(i * 16, 16), 16)
        grad = norm_grad(nin[at], iin[at], rows16(first_l, i))
        out[at] = (gmid[at].astype(F32) + grad).astype(BF)
        return c

    lax.fori_loop(0, 16, grad_norm_in, 0)

    tm_sent(0, tok, home_part, tok_t, time_part)
    tm_sent(1, blend_s, time_part, blend_h, home_part)
    tm_sent(2, mix_s, home_part, mix_l, time_part)
    tm_sent(3, first_s, time_part, first_l, home_part)
    sp_sent(3, g_s, g_l, 64)
    sp_sent(0, k_s, k_l, 128)
    sp_sent(1, v_s, v_l, 128)
    sp_sent(2, q_s, q_l, 64)
    back_sent(0, gq_a, gq_l, 64)
    back_sent(1, gk_a, gk_l, 128)
    back_sent(2, gv_a, gv_l, 128)


def on_device(tokens, grad_out, *weights):
    bf = lambda *shape: pltpu.VMEM(shape, BF)
    f32 = lambda *shape: pltpu.VMEM(shape, F32)
    dma = pltpu.SemaphoreType.DMA
    tall, flat = bf(D, HW), bf(HW, D)
    any_space = pl.BlockSpec(memory_space=pl.ANY)
    out = pl.pallas_call(
        kernel,
        out_shape=jax.ShapeDtypeStruct((256, D), BF),
        in_specs=[any_space] * 10,
        out_specs=pl.BlockSpec(memory_space=pltpu.VMEM),
        scratch_shapes=[
            tall, tall, tall, flat, tall, tall, tall, flat,
            bf(2, 16, 8, D), bf(256, D), bf(32, 8, D), f32(256, D), f32(256, 1), bf(256, D),
            bf(6, 256, 128), bf(6, 256, 128), bf(6, 256, 128), f32(6, 256, 256), bf(6, 256, 128),
            bf(32, 8, HW), bf(2, 16, 8, HW), bf(256, D), f32(256, D), f32(256, 1),
            bf(2, 6, 128, 128), bf(2, 6, 128, 128), bf(2, 6, 128, 128), bf(2, 6, 128, 128),
            bf(2, 1024, 128), bf(2, 1024, 128), bf(1536, 128), bf(1536, 128),
            bf(1536, 128), f32(2, 1024, 128), f32(2, 1024, 128), bf(2, 1024, 128), bf(2, 1024, 128),
            bf(2, 6, 128, 128), bf(2, 8, 128, 128), bf(2, 8, 128, 128),
            f32(256, D), bf(256, D), bf(2, 16, 8, HW), bf(32, 8, HW), bf(3, 256, HW),
            bf(32, 8, D), bf(2, 16, 8, D),
            dma((10,)), dma((4, 16)), dma((4, 16)), dma((4, 2, 8)), dma((4, 2, 8)), dma((3, 2, 8)), dma((3, 2, 8)),
        ],
        compiler_params=pltpu.CompilerParams(
            collective_id=0, has_side_effects=True, vmem_limit_bytes=60 * 2**20
        ),
    )(tokens.reshape(2, 16, 8, D), grad_out.reshape(256, D), *weights)
    return out.reshape(1, 2, 128, D)


def solution(mesh):
    row = P(None, "tm", "space", None)
    return jax.shard_map(
        on_device,
        mesh=mesh,
        in_specs=(row, row) + (P(),) * 8,
        out_specs=row,
        check_vma=False,
    )
```

time: 251 us -> 122 us (0.49)
  Pallas kernels: 0 us -> 120 us
  blocking collectives: 68.6 us -> 0 us
  matrix products: 57.7 us -> 0 us
  local copies, waits for them, and re-layouts: 51.6 us -> 2.06 us
  waiting for transfers between devices: 31.9 us -> 0 us
  starting transfers between devices: 19.9 us -> 0 us
  other arithmetic: 18.6 us -> 0 us
    pallas_call x0 -> x1, Pallas kernels: none -> 120 us  [on_device(): pl.pallas_call(kernel, out_shape=jax.ShapeDtypeStruct((256, D), BF), in_s...]
    all_to_all x3 -> x0, blocking collectives: 68.6 us -> none  [the longest x1 29.2 us: to_heads(): moved = lax.all_to_all(padded, 'space', 0, 0, tiled=True)]
    dot_general x25 -> x0, matrix products: 47.8 us -> none  [the longest x7 19 us: mm(): return jnp.dot(left, right, preferred_element_type=F32)]
    all_to_all x3 -> x0, waiting for transfers between devices: 31.9 us -> none  [the longest x2 18.6 us: to_home(): moved = lax.all_to_all(rows.reshape(32, 8, width), 'tm', 0, 1, tiled=True)]
    all_to_all x3 -> x0, starting transfers between devices: 19.9 us -> none  [the longest x2 10.5 us: to_home(): moved = lax.all_to_all(rows.reshape(32, 8, width), 'tm', 0, 1, tiled=True)]
    convert_element_type x10 -> x0, local copies, waits for them, and re-layouts: 14.1 us -> none  [the longest x3 5.76 us: on_device(): mm(second_rows, w).astype(BF)]
    convert_element_type x7 -> x0, other arithmetic: 12 us -> none  [the longest x1 4.72 us: forward(): blend = ein('glm,gmx->glx', shares.astype(BF), value).astype(BF)]
    reshape x3 -> x0, local copies, waits for them, and re-layouts: 10.5 us -> none  [the longest x2 10.1 us: to_heads(): moved = moved.reshape(8, len(members), 2, 128, HD).transpose(1, 2, 0, 3, 4)]
  transfers between devices with their start and end apart: 3 -> 0, of which waited for: 3 -> 0; matrix products, arithmetic and copies ran while one was open for 2% -> 0% of each run, Pallas kernels for 0% -> 0%
where the time goes in v2:
time: 122 us
  Pallas kernels  120 us (98%)
  local copies, waits for them, and re-layouts  2.06 us (2%)
    pallas_call x1, Pallas kernels, on_device(): pl.pallas_call(kernel, out_shape=jax.ShapeDtypeStruct((256, D), BF), in_s...  120 us

profile of v2, /device:TPU:1, one launch (start us, length us, event | category | flops | bytes accessed | tf_op | source)
XLA Modules:
  0.0 122.1 jit_solution(3161147715230254230)
XLA Ops:
  0.0 120.1 %shard_map.100 = bf16[256,1536]{1,0:T(8,128)(2,1)} custom-call(bf16[2,16,8,1536]{3,2,1,0:T(8,128)(2,1)} %bitcast.4, bf16[256,1536]{1,0:T(8,128)(2,1)} %bitcast.5, bf16[1536,768]{1,0:T(8,128)(2,1)} %tq.1, bf16[1536,768]{1,0:T(8,128)(2,1)} %tk.1, bf16[1536,768]{1,0:T(8,128)(2,1)} %tv.1, bf16[768,1536]{1,0:T(8,128)(2,1)} %to.1, bf16[1536,768]{1,0:T(8,128)(2,1)} %sq.1, ...), custom_call_target="tpu_custom_call" | custom-call | tf_op jit(solution)/shard_map/pallas_call | solution.py:400
  120.1 2.1 %copy.12 = bf16[1,2,128,1536]{3,2,1,0:T(8,128)(2,1)} copy(bf16[1,2,128,1536]{3,2,1,0:T(8,128)(2,1)} %bitcast.3) | data formatting | bytes 1572864

commit v3 on v2

--- a/solution.py
+++ b/solution.py
@@ -15,6 +15,8 @@
 D = 1536
 HW = 768
 MESH = pl.DeviceIdType.MESH
+BOTH = ((0, True), (1, False))
+WHOLE, HALF = BOTH[:1], BOTH[1:]
 
 
 def mm(left, right):
@@ -69,9 +71,6 @@
             (to, w_to), (sk, w_sk), (sv, w_sv), (sq, w_sq),
         ))
     ]
-    for load in loads:
-        load.start()
-
     barrier = pltpu.get_barrier_semaphore()
 
     def greet_t(k, c):
@@ -138,40 +137,40 @@
             return ref.at[pl.ds(pl.multiple_of(n * 128, 128), 128)]
         return ref.at[pl.ds(pl.multiple_of(1024 + n * 64, 64), 64)]
 
-    def sp_copies(which, src, dst, peer, rows):
+    def sp_copies(which, src, dst, peer, rows, kinds):
         return [
             pltpu.make_async_remote_copy(
                 src_ref=slab(src, peer, whole, rows), dst_ref=stripe(dst, me_s, whole, rows),
                 send_sem=sp_send.at[which, kind, peer], recv_sem=sp_recv.at[which, kind, me_s],
                 device_id={"space": peer}, device_id_type=MESH)
-            for kind, whole in enumerate((True, False))
+            for kind, whole in kinds
         ]
 
-    def sp_start(which, src, dst, rows):
-        for kind, whole in enumerate((True, False)):
+    def sp_start(which, src, dst, rows, kinds=BOTH):
+        for kind, whole in kinds:
             pltpu.make_async_copy(
                 slab(src, me_s, whole, rows), stripe(dst, me_s, whole, rows), sp_recv.at[which, kind, me_s]
             ).start()
 
         def go(k, c):
-            for copy in sp_copies(which, src, dst, (me_s + k) % 8, rows):
+            for copy in sp_copies(which, src, dst, (me_s + k) % 8, rows, kinds):
                 copy.start()
             return c
 
         lax.fori_loop(1, 8, go, 0)
 
-    def sp_wait(which, dst, rows):
+    def sp_wait(which, dst, rows, kinds=BOTH):
         def go(n, c):
-            for kind, whole in enumerate((True, False)):
+            for kind, whole in kinds:
                 part = stripe(dst, n, whole, rows)
                 pltpu.make_async_copy(part, part, sp_recv.at[which, kind, n]).wait()
             return c
 
         lax.fori_loop(0, 8, go, 0)
 
-    def sp_sent(which, src, dst, rows):
-        def go(k, c):
-            for copy in sp_copies(which, src, dst, (me_s + k) % 8, rows):
+    def sp_sent(which, src, dst, rows, kinds=BOTH):
+        def go(k, c):
+            for copy in sp_copies(which, src, dst, (me_s + k) % 8, rows, kinds):
                 copy.wait_send()
             return c
 
@@ -184,40 +183,40 @@
             return ref.at[n // 4, 4 + (n % 4) // 2, pl.ds(pl.multiple_of((n % 2) * 64, 64), 64)]
         return ref.at[n // 4, 4 + n % 4]
 
-    def back_copies(which, src, dst, peer, rows):
+    def back_copies(which, src, dst, peer, rows, kinds):
         return [
             pltpu.make_async_remote_copy(
                 src_ref=stripe(src, peer, whole, rows), dst_ref=home_slot(dst, me_s, whole, rows),
                 send_sem=back_send.at[which, kind, peer], recv_sem=back_recv.at[which, kind, me_s],
                 device_id={"space": peer}, device_id_type=MESH)
-            for kind, whole in enumerate((True, False))
+            for kind, whole in kinds
         ]
 
-    def back_start(which, src, dst, rows):
-        for kind, whole in enumerate((True, False)):
+    def back_start(which, src, dst, rows, kinds=BOTH):
+        for kind, whole in kinds:
             pltpu.make_async_copy(
                 stripe(src, me_s, whole, rows), home_slot(dst, me_s, whole, rows), back_recv.at[which, kind, me_s]
             ).start()
 
         def go(k, c):
-            for copy in back_copies(which, src, dst, (me_s + k) % 8, rows):
+            for copy in back_copies(which, src, dst, (me_s + k) % 8, rows, kinds):
                 copy.start()
             return c
 
         lax.fori_loop(1, 8, go, 0)
 
-    def back_wait(which, dst, rows):
+    def back_wait(which, dst, rows, kinds=BOTH):
         def go(n, c):
-            for kind, whole in enumerate((True, False)):
+            for kind, whole in kinds:
                 part = home_slot(dst, n, whole, rows)
                 pltpu.make_async_copy(part, part, back_recv.at[which, kind, n]).wait()
             return c
 
         lax.fori_loop(0, 8, go, 0)
 
-    def back_sent(which, src, dst, rows):
-        def go(k, c):
-            for copy in back_copies(which, src, dst, (me_s + k) % 8, rows):
+    def back_sent(which, src, dst, rows, kinds=BOTH):
+        def go(k, c):
+            for copy in back_copies(which, src, dst, (me_s + k) % 8, rows, kinds):
                 copy.wait_send()
             return c
 
@@ -229,11 +228,12 @@
                 ref[t, h] = flat[t * 128:(t + 1) * 128, h * 128:(h + 1) * 128]
 
     tm_start(0, tok, home_part, tok_t, time_part)
+    for load in loads:
+        load.start()
 
     loads[0].wait()
     loads[1].wait()
     put_heads(g_s, mmt(gout_v[...], w_so[...]).astype(BF))
-    sp_start(3, g_s, g_l, 64)
 
     loads[2].wait()
 
@@ -246,14 +246,16 @@
 
     lax.fori_loop(0, 16, norm_home, 0)
 
-    tm_wait(0, tok_t, time_part)
-
-    def norm_time(i, c):
-        normed, _ = layer_stats(tok_t[pl.ds(i * 2, 2)].astype(F32).reshape(16, D))
-        rows_b[pl.ds(pl.multiple_of(i * 16, 16), 16)] = normed.astype(BF)
+    def norm_time(k, c):
+        n = (me_t + k) % 16
+        part = time_part(tok_t, n)
+        pltpu.make_async_copy(part, part, tm_recv.at[0, n]).wait()
+        normed, _ = layer_stats(tok_t[pl.ds(n * 2, 2)].astype(F32).reshape(16, D))
+        rows_b[pl.ds(pl.multiple_of(n * 16, 16), 16)] = normed.astype(BF)
         return c
 
     lax.fori_loop(0, 16, norm_time, 0)
+    sp_start(3, g_s, g_l, 64)
     for n, (weight, dst) in enumerate(((w_tq, q_t), (w_tk, k_t), (w_tv, v_t))):
         loads[3 + n].wait()
         flat = mm(rows_b[...], weight[...]).astype(BF)
@@ -293,12 +295,10 @@
     )):
         loads[7 + n].wait()
         put_heads(src, mm(rows_b[...], weight[...]).astype(BF))
-        sp_start(n, src, dst, rows)
-
-    sp_wait(3, g_l, 64)
-    sp_wait(0, k_l, 128)
-    sp_wait(1, v_l, 128)
-    sp_wait(2, q_l, 64)
+        sp_start(n, src, dst, rows, WHOLE)
+    for n, (src, dst, rows) in enumerate(((k_s, k_l, 128), (v_s, v_l, 128), (q_s, q_l, 64))):
+        sp_start(n, src, dst, rows, HALF)
+
     gk_f[...] = jnp.zeros_like(gk_f)
     gv_f[...] = jnp.zeros_like(gv_f)
 
@@ -318,28 +318,32 @@
         gv_f[u] += tmm(rounded, mix)
         return c
 
-    lax.fori_loop(0, 6, attend, 0)
-    back_start(0, gq_a, gq_l, 64)
-    gk_a[...] = gk_f[...].astype(BF)
-    back_start(1, gk_a, gk_l, 128)
-    gv_a[...] = gv_f[...].astype(BF)
-    back_start(2, gv_a, gv_l, 128)
+    for u, kinds in enumerate((WHOLE, HALF)):
+        sp_wait(3, g_l, 64, kinds)
+        sp_wait(0, k_l, 128, kinds)
+        sp_wait(1, v_l, 128, kinds)
+        sp_wait(2, q_l, 64, kinds)
+        lax.fori_loop(4 * u, 4 + 2 * u, attend, 0)
+        back_start(0, gq_a, gq_l, 64, kinds)
+        gk_a[u] = gk_f[u].astype(BF)
+        back_start(1, gk_a, gk_l, 128, kinds)
+        gv_a[u] = gv_f[u].astype(BF)
+        back_start(2, gv_a, gv_l, 128, kinds)
 
     def take(ref, h):
         return ref[:, h].reshape(256, 128)
 
-    def joined(ref):
-        parts = [take(ref, h) for h in range(4)]
-        for h in (4, 6):
-            parts.append((take(ref, h).astype(F32) + take(ref, h + 1).astype(F32)).astype(BF))
-        return jnp.concatenate(parts, axis=-1)
-
-    back_wait(0, gq_l, 64)
-    acc[...] = mmt(jnp.concatenate([take(gq_l, h) for h in range(6)], axis=-1), w_sq[...])
-    back_wait(1, gk_l, 128)
-    acc[...] += mmt(joined(gk_l), w_sk[...])
-    back_wait(2, gv_l, 128)
-    acc[...] += mmt(joined(gv_l), w_sv[...])
+    def added(ref, h):
+        return (take(ref, h).astype(F32) + take(ref, h + 1).astype(F32)).astype(BF)
+
+    acc[...] = jnp.zeros_like(acc)
+    for which, (ref, weight) in enumerate(((gq_l, w_sq), (gk_l, w_sk), (gv_l, w_sv))):
+        back_wait(which, ref, 64 if which == 0 else 128, WHOLE)
+        acc[...] += mmt(jnp.concatenate([take(ref, h) for h in range(4)], axis=-1), weight[:, :512])
+    for which, (ref, weight) in enumerate(((gq_l, w_sq), (gk_l, w_sk), (gv_l, w_sv))):
+        back_wait(which, ref, 64 if which == 0 else 128, HALF)
+        last = (take(ref, 4), take(ref, 5)) if which == 0 else (added(ref, 4), added(ref, 6))
+        acc[...] += mmt(jnp.concatenate(last, axis=-1), weight[:, 512:])
 
     def grad_norm_mid(i, c):
         at = pl.ds(pl.multiple_of(i * 16, 16), 16)
@@ -363,25 +367,27 @@
         tg[0, :, cols] = mm(grads, k_t[h]).astype(BF)
         tg[1, :, cols] = tmm(grads, q_t[h]).astype(BF)
         tg[2, :, cols] = tmm(shares.astype(BF), mix).astype(BF)
-    acc[...] = mmt(tg[0], w_tq[...])
-    acc[...] += mmt(tg[1], w_tk[...])
-    acc[...] += mmt(tg[2], w_tv[...])
-    first_s[...] = acc[...].reshape(32, 8, D).astype(BF)
-    tm_start(3, first_s, time_part, first_l, home_part)
-    tm_wait(3, first_l, home_part)
-
-    def grad_norm_in(i, c):
+    for c in range(3):
+        cols = slice(c * 512, (c + 1) * 512)
+        part = mmt(tg[0], w_tq[cols]) + mmt(tg[1], w_tk[cols]) + mmt(tg[2], w_tv[cols])
+        first_s[c] = part.reshape(32, 8, 512).astype(BF)
+        tm_start(3 + c, first_s.at[c], time_part, first_l.at[c], home_part)
+    for c in range(3):
+        tm_wait(3 + c, first_l.at[c], home_part)
+
+    def grad_norm_in(i, z):
         at = pl.ds(pl.multiple_of(i * 16, 16), 16)
-        grad = norm_grad(nin[at], iin[at], rows16(first_l, i))
+        grad = norm_grad(nin[at], iin[at], jnp.concatenate([rows16(first_l.at[c], i) for c in range(3)], axis=-1))
         out[at] = (gmid[at].astype(F32) + grad).astype(BF)
-        return c
+        return z
 
     lax.fori_loop(0, 16, grad_norm_in, 0)
 
     tm_sent(0, tok, home_part, tok_t, time_part)
     tm_sent(1, blend_s, time_part, blend_h, home_part)
     tm_sent(2, mix_s, home_part, mix_l, time_part)
-    tm_sent(3, first_s, time_part, first_l, home_part)
+    for c in range(3):
+        tm_sent(3 + c, first_s.at[c], time_part, first_l.at[c], home_part)
     sp_sent(3, g_s, g_l, 64)
     sp_sent(0, k_s, k_l, 128)
     sp_sent(1, v_s, v_l, 128)
@@ -412,8 +418,8 @@
             bf(1536, 128), f32(2, 1024, 128), f32(2, 1024, 128), bf(2, 1024, 128), bf(2, 1024, 128),
             bf(2, 6, 128, 128), bf(2, 8, 128, 128), bf(2, 8, 128, 128),
             f32(256, D), bf(256, D), bf(2, 16, 8, HW), bf(32, 8, HW), bf(3, 256, HW),
-            bf(32, 8, D), bf(2, 16, 8, D),
-            dma((10,)), dma((4, 16)), dma((4, 16)), dma((4, 2, 8)), dma((4, 2, 8)), dma((3, 2, 8)), dma((3, 2, 8)),
+            bf(3, 32, 8, 512), bf(3, 2, 16, 8, 512),
+            dma((10,)), dma((6, 16)), dma((6, 16)), dma((4, 2, 8)), dma((4, 2, 8)), dma((3, 2, 8)), dma((3, 2, 8)),
         ],
         compiler_params=pltpu.CompilerParams(
             collective_id=0, has_side_effects=True, vmem_limit_bytes=60 * 2**20

time: 122 us -> 110 us (0.902)
  Pallas kernels: 120 us -> 108 us
    pallas_call x1, Pallas kernels: 120 us -> 108 us  [on_device(): pl.pallas_call(kernel, out_shape=jax.ShapeDtypeStruct((256, D), BF), in_s...]
where the time goes in v3:
time: 110 us
  Pallas kernels  108 us (98%)
  local copies, waits for them, and re-layouts  2.06 us (2%)
    pallas_call x1, Pallas kernels, on_device(): pl.pallas_call(kernel, out_shape=jax.ShapeDtypeStruct((256, D), BF), in_s...  108 us

profile of v3, /device:TPU:1, one launch (start us, length us, event | category | flops | bytes accessed | tf_op | source)
XLA Modules:
  0.0 110.3 jit_solution(7881419509326968599)
XLA Ops:
  0.0 108.3 %shard_map.100 = bf16[256,1536]{1,0:T(8,128)(2,1)} custom-call(bf16[2,16,8,1536]{3,2,1,0:T(8,128)(2,1)} %bitcast.4, bf16[256,1536]{1,0:T(8,128)(2,1)} %bitcast.5, bf16[1536,768]{1,0:T(8,128)(2,1)} %tq.1, bf16[1536,768]{1,0:T(8,128)(2,1)} %tk.1, bf16[1536,768]{1,0:T(8,128)(2,1)} %tv.1, bf16[768,1536]{1,0:T(8,128)(2,1)} %to.1, bf16[1536,768]{1,0:T(8,128)(2,1)} %sq.1, ...), custom_call_target="tpu_custom_call" | custom-call | tf_op jit(solution)/shard_map/pallas_call | solution.py:406
  108.3 2.1 %copy.12 = bf16[1,2,128,1536]{3,2,1,0:T(8,128)(2,1)} copy(bf16[1,2,128,1536]{3,2,1,0:T(8,128)(2,1)} %bitcast.3) | data formatting | bytes 1572864
